TPU v7x, 256 devices: a whole 4x4x8 slice. The times are simulated.
256 devices in a mesh: row: 32 (over y, z), col: 8 (over x, core).
Axes of the slice: x: 4, y: 4, z: 8, core: 2. Of those that a mesh axis runs over, the one named last changes fastest.
Arguments:
- load_currents: float32 [16, 256, 128, 128], P(None, 'row', 'col'), may hold values from -24 to 24
- block_library: float32 [8, 128, 128], replicated, may hold values from -4.0625 to 24.1, as said below
- strap_conductance: float32 [2, 128], replicated, may hold values from 0.5 to 4
- block_types: int32 [256, 128], P('row', 'col'), may hold values from 0 to 7
- aggregate_map: int32 [256, 128], P('row', 'col'), may hold values from 0 to 255, as said below
Outputs:
- node_voltage: float32 [16, 256, 128, 128], P(None, 'row', 'col')
- residual: float32 [16, 256, 128, 128], P(None, 'row', 'col')
Inputs may be any that keep to these rules, and one draw needn't show every extreme that they name: `aggregate_map`: each aggregate id names an aggregate of one column group of 16 block columns; the same id in another column group is another aggregate. Every aggregate of every column group holds at least one block. `block_library`: each library block is symmetric positive definite, with nonpositive off-diagonal entries and positive row sums.
All inputs are finite; a program needn't handle non-finite values.
Results may differ from a plain program's by a relative error of at most 0.0003.
Values sent between devices are 32-bit elements; how exact they have to be, the bound alone decides.
A program may use at most 64 MiB of HBM per device.

v0:
```python
import jax
import jax.numpy as jnp
from jax import lax
from jax.sharding import PartitionSpec as P

SWEEPS = 3
ITERS = 2
AGR = 4
AGC = 4


def padded_2(array, sides, width):
    for axis, dim in sides:
        size, length = (lax.axis_size(axis), array.shape[dim])
        up = [(i, (i + 1) % size) for i in range(size - 1)]
        down = [(j, i) for i, j in up]
        last = lax.slice_in_dim(array, length - width, length, axis=dim)
        first = lax.slice_in_dim(array, 0, width, axis=dim)
        before = lax.ppermute(last, axis, up)
        after = lax.ppermute(first, axis, down)
        array = jnp.concatenate([before, array, after], axis=dim)
    return array


def from_behind(array, axis, by):
    length = lax.axis_size(axis)
    pairs = [(i, i + by) for i in range(length) if 0 <= i + by < length]
    return lax.ppermute(array, axis, pairs)


def coarse_terms(group_ids, group_types, block_sums, north_weight, east_weight, count):
    centre = block_sums[group_types] + 2.0 * north_weight + 2.0 * east_weight
    flat = group_ids.reshape(-1)
    upper = group_ids[:-1].reshape(-1)
    lower = group_ids[1:].reshape(-1)
    left = group_ids[:, :-1].reshape(-1)
    right = group_ids[:, 1:].reshape(-1)
    index = jnp.concatenate(
        [
            flat * count + flat,
            upper * count + lower,
            lower * count + upper,
            left * count + right,
            right * count + left,
        ]
    )
    values = jnp.concatenate(
        [
            centre.reshape(-1),
            -north_weight * jnp.ones((2 * upper.shape[0],), jnp.float32),
            -east_weight * jnp.ones((2 * left.shape[0],), jnp.float32),
        ]
    )
    return jax.ops.segment_sum(values, index, num_segments=count * count).reshape(count, count)


def alignment_sum(residual, zeta):
    return lax.psum(jnp.sum(residual * zeta, axis=(1, 2, 3)), ("row", "col"))


def on_device(load_currents, block_library, strap_conductance, block_types, aggregate_map):
    sizings, rows_local, cols_local, nodes = load_currents.shape
    blocks = rows_local * cols_local
    count = rows_local * lax.axis_size("row") // AGR * (cols_local // AGC)
    picked = block_library[block_types.reshape(-1)]
    couple = 2.0 * strap_conductance[0] + 2.0 * strap_conductance[1]
    diag_library = jnp.diagonal(block_library, axis1=1, axis2=2)
    diagonal = diag_library[block_types] + couple
    block_sums = jnp.sum(block_library, axis=(1, 2))
    north_weight = jnp.sum(strap_conductance[0])
    east_weight = jnp.sum(strap_conductance[1])

    def block_products(field):
        flat = field.reshape(sizings, blocks, nodes)
        product = jnp.einsum("bij,sbj->sbi", picked, flat, precision=lax.Precision.HIGHEST)
        return product.reshape(sizings, rows_local, cols_local, nodes)

    local_matrix = coarse_terms(
        aggregate_map, block_types, block_sums, north_weight, east_weight, count
    )
    below_ids = from_behind(aggregate_map[0], "row", -1)
    present = (lax.axis_index("row") < lax.axis_size("row") - 1).astype(jnp.float32)
    bottom_ids = aggregate_map[-1]
    cross_index = jnp.concatenate([bottom_ids * count + below_ids, below_ids * count + bottom_ids])
    cross_values = -north_weight * present * jnp.ones((2 * cols_local,), jnp.float32)
    cross_matrix = jax.ops.segment_sum(
        cross_values, cross_index, num_segments=count * count
    ).reshape(count, count)
    coarse_matrix = lax.psum(local_matrix + cross_matrix, "row")
    factor = jnp.linalg.cholesky(coarse_matrix)
    flat_ids = aggregate_map.reshape(-1)

    def smooth(residual):
        result = residual / diagonal
        for sweep in range(SWEEPS - 1):
            image = block_products(result) + couple * result
            result = result + (residual - image) / diagonal
        return result

    def coarse_part(residual):
        sums = residual.sum(-1).reshape(sizings, blocks).T
        local = jax.ops.segment_sum(sums, flat_ids, num_segments=count)
        gathered = lax.psum(local, "row")
        solved = jax.scipy.linalg.cho_solve((factor, True), gathered)
        return solved[flat_ids].T.reshape(sizings, rows_local, cols_local)[..., None]

    def precondition(residual):
        return smooth(residual) + coarse_part(residual)

    node_voltage = jnp.zeros_like(load_currents)
    residual = load_currents
    zeta = precondition(residual)
    direction = zeta
    aligned = alignment_sum(residual, zeta)
    for iteration in range(ITERS):
        padded = padded_2(direction, (("row", 1), ("col", 2)), 1)
        north = padded[:, :-2, 1:-1]
        south = padded[:, 2:, 1:-1]
        west = padded[:, 1:-1, :-2]
        east = padded[:, 1:-1, 2:]
        lateral = strap_conductance[0] * (2.0 * direction - north - south) + strap_conductance[
            1
        ] * (2.0 * direction - west - east)
        image = block_products(direction) + lateral
        curvature = lax.psum(jnp.sum(direction * image, axis=(1, 2, 3)), ("row", "col"))
        step_size = (aligned / curvature)[:, None, None, None]
        node_voltage = node_voltage + step_size * direction
        residual = residual - step_size * image
        if iteration + 1 < ITERS:
            zeta = precondition(residual)
            fresh = alignment_sum(residual, zeta)
            blend = (fresh / aligned)[:, None, None, None]
            direction = zeta + blend * direction
            aligned = fresh
    return (node_voltage, residual)


def solution(mesh):
    placed = (P(None, "row", "col", None), P(), P(), P("row", "col"), P("row", "col"))
    return jax.shard_map(
        on_device,
        mesh=mesh,
        in_specs=placed,
        out_specs=(P(None, "row", "col", None), P(None, "row", "col", None)),
        check_vma=False,
    )
```

profile of v0, /device:TPU:1, one launch (start us, length us, event | category | flops | bytes accessed | tf_op | source)
XLA Modules:
  0.0 772.2 jit_solution(3687097905419126397)
XLA Ops:
  8.0 1.3 collective-permute-start
  9.3 1.4 slice_reduce_fusion.1
  18.7 5.9 copy.47
  25.0 1.8 gather_fusion
  26.8 1.2 gather_fusion.3
  28.8 4.3 gather_fusion.2
  33.8 16.3 %fusion.50 = f32[128,16,128]{2,1,0:T(8,128)S(1)} fusion(f32[16,128,128]{2,0,1:T(8,128)S(1)} %bitcast.139, f32[128,128,128]{2,1,0:T(8,128)} %gather_fusion.2), kind=kOutput, calls=%fused_computation.144 | convolution fusion | flops 402653184 | bytes 10485760 | tf_op jit(solution)/shard_map/bij,sbj->sbi/dot_general | solution.py:75
  50.8 14.2 %fusion.51 = f32[128,16,128]{2,1,0:T(8,128)} fusion(f32[16,128,128]{2,0,1:T(8,128)S(1)} %bitcast.140, f32[128,128,128]{2,1,0:T(8,128)S(1)} %bitcast.127), kind=kOutput, calls=%fused_computation.145 | convolution fusion | flops 402653184 | bytes 10485760 | tf_op jit(solution)/shard_map/bij,sbj->sbi/dot_general | solution.py:75
  66.2 4.7 scatter_custom_fusion
  72.3 1.7 scatter_custom_fusion.1
  74.0 120.5 %psum.50 = f32[256,16]{0,1:T(8,128)S(1)} all-reduce(f32[256,16]{0,1:T(8,128)S(1)} %copy.55), channel_id=1, replica_groups=mesh['row'=32,'col'=8] {'row'}, use_global_device_ids=true, to_apply=%region_11.12 | all-reduce | flops 4096 | bytes 32768 | tf_op jit(solution)/shard_map/psum | solution.py:103
  194.5 23.7 %all-reduce.5.cloned.1.call-done = f32[256,256]{0,1:T(8,128)} async-done(((f32[256,256]{0,1:T(8,128)}), f32[256,256]{0,1:T(8,128)}) %all-reduce.5.cloned.1.call-update) | async-done | bytes 262160 | tf_op jit(solution)/shard_map/psum | solution.py:89
  218.2 1.1 copy.53
  220.3 11.7 %cholesky.50 = f32[128,128]{1,0:T(8,128)S(1)} custom-call(f32[128,128]{1,0:T(8,128)S(1)} %cholesky.118), custom_call_target="Cholesky" | custom-call | tf_op jit(solution)/shard_map/jit(cholesky)/cholesky | solution.py:90
  232.1 9.8 %custom-call.16 = f32[1,128,128]{1,2,0:T(8,128)S(1)} custom-call(f32[1,128,128]{2,1,0:T(8,128)S(1)} %get-tuple-element.55), custom_call_target="InvertDiagBlocksLowerTriangular" | custom-call | tf_op jit(solution)/shard_map/jit(cholesky)/cholesky | solution.py:90
  242.4 11.7 %cholesky.105 = f32[128,128]{1,0:T(8,128)S(1)} custom-call(f32[128,128]{1,0:T(8,128)S(1)} %convolution_subtract_fusion), custom_call_target="Cholesky" | custom-call | tf_op jit(solution)/shard_map/jit(cholesky)/cholesky | solution.py:90
  256.1 3.8 while.4
  256.7 1.3 bitcast_dynamic-update-slice_fusion.2
  258.6 1.3 bitcast_dynamic-update-slice_fusion.2
  260.0 19.8 %custom-call.20 = f32[2,128,128]{1,2,0:T(8,128)S(1)} custom-call(f32[2,128,128]{2,1,0:T(8,128)S(1)} %get-tuple-element.17), custom_call_target="InvertDiagBlocksLowerTriangular" | custom-call | tf_op jit(solution)/shard_map/jit(_cho_solve)/triangular_solve | solution.py:104
  281.8 2.0 add_add_fusion.1
  283.8 1.9 collective-permute-start.1
  285.7 1.3 collective-permute-start.2
  287.6 4.0 collective-permute-done.2
  291.6 9.7 %collective-permute-start.3 = (f32[16,10,1,128]{3,0,2,1:T(8,128)S(1)}, f32[16,10,1,128]{3,0,2,1:T(8,128)S(1)}, u32[]{:S(2)}, u32[]{:S(2)}) collective-permute-start(f32[16,10,1,128]{3,0,2,1:T(8,128)S(1)} %get-tuple-element.44), channel_id=1, source_target_pairs={{0,1},{1,2},{2,3},{3,4},{4,5},{5,6},{6,7},{8,9},{9,10},{10,11},{11... | collective-permute-start | bytes 245768 | tf_op jit(solution)/shard_map/ppermute | solution.py:19
  301.4 1.9 collective-permute-start.4
  303.3 15.4 %fusion.52 = f32[128,16,128]{2,1,0:T(8,128)S(1)} fusion(f32[16,128,128]{2,0,1:T(8,128)S(1)} %bitcast.130, f32[128,128,128]{2,1,0:T(8,128)} %gather_fusion.2), kind=kOutput, calls=%fused_computation.146 | convolution fusion | flops 402653184 | bytes 10485760 | tf_op jit(solution)/shard_map/bij,sbj->sbi/dot_general | solution.py:75
  318.7 1.8 multiply_reduce_fusion.2
  320.5 77.0 %all-reduce.2 = (f32[16]{0:T(128)S(1)}, f32[16]{0:T(128)S(1)}) all-reduce(f32[16]{0:T(128)S(1)} %get-tuple-element.22, f32[16]{0:T(128)S(1)} %get-tuple-element.21), channel_id=1, replica_groups=mesh['row'=32,'col'=8] {'row','col'}, use_global_device_ids=true, to_apply=%region_13.15 | all-reduce | flops 32 | bytes 256 | tf_op jit(solution)/shard_map/psum | solution.py:58
  397.6 2.1 broadcast_divide_fusion
  399.7 15.8 %divide_add_fusion = (f32[16,8,16,128]{3,0,2,1:T(8,128)S(1)}, f32[16,8,16]{0,2,1:T(8,128)S(1)}, f32[128,16,128]{2,1,0:T(8,128)S(1)}) fusion(f32[16,8,16,128]{3,0,2,1:T(8,128)S(1)} %get-tuple-element.38, f32[128]{0:T(128)S(1)} %add_multiply_fusion, f32[8,16,128]{2,1,0:T(8,128)S(1)} %broadcast_add_fusion, f32[16,128,128]{2,0,1:T(8,128)S(1)} %bitcast.137, ...), kind=kOutput, calls=%fused_computation.54 | convolution fusion | flops 404486144 | bytes 12657152 | tf_op jit(solution)/shard_map/bij,sbj->sbi/dot_general | solution.py:75
  415.5 14.0 %fusion.53 = f32[128,16,128]{2,1,0:T(8,128)} fusion(f32[16,128,128]{2,0,1:T(8,128)S(1)} %bitcast.138, f32[128,128,128]{2,1,0:T(8,128)S(1)} %bitcast.129), kind=kOutput, calls=%fused_computation.147 | convolution fusion | flops 402653184 | bytes 10485760 | tf_op jit(solution)/shard_map/bij,sbj->sbi/dot_general | solution.py:75
  429.6 1.9 scatter_custom_fusion.2
  432.4 110.3 %psum.53 = f32[256,16]{0,1:T(8,128)S(1)} all-reduce(f32[256,16]{0,1:T(8,128)S(1)} %copy.61), channel_id=1, replica_groups=mesh['row'=32,'col'=8] {'row'}, use_global_device_ids=true, to_apply=%region_18.20 | all-reduce | flops 4096 | bytes 32768 | tf_op jit(solution)/shard_map/psum | solution.py:103
  548.0 1.9 multiply_reduce_fusion.1
  549.9 100.2 %psum.54 = f32[16]{0:T(128)S(1)} all-reduce(f32[16]{0:T(128)S(1)} %multiply_reduce_fusion.1), channel_id=1, replica_groups=mesh['row'=32,'col'=8] {'row','col'}, use_global_device_ids=true, to_apply=%region_20.22 | all-reduce | flops 16 | bytes 128 | tf_op jit(solution)/shard_map/psum | solution.py:58
  650.7 2.1 multiply_add_fusion.1
  652.8 3.7 collective-permute-start.5
  656.5 1.3 collective-permute-start.6
  658.7 3.6 collective-permute-done.6
  662.3 4.3 collective-permute-start.7
  666.5 1.9 collective-permute-start.8
  668.5 15.4 %fusion.54 = f32[128,16,128]{2,1,0:T(8,128)S(1)} fusion(f32[16,128,128]{2,0,1:T(8,128)S(1)} %bitcast.131, f32[128,128,128]{2,1,0:T(8,128)} %gather_fusion.2), kind=kOutput, calls=%fused_computation.148 | convolution fusion | flops 402653184 | bytes 10485760 | tf_op jit(solution)/shard_map/bij,sbj->sbi/dot_general | solution.py:75
  683.9 1.5 multiply_reduce_fusion
  685.3 75.4 %psum.55 = f32[16]{0:T(128)S(1)} all-reduce(f32[16]{0:T(128)S(1)} %get-tuple-element.35), channel_id=1, replica_groups=mesh['row'=32,'col'=8] {'row','col'}, use_global_device_ids=true, to_apply=%region_22.24 | all-reduce | flops 16 | bytes 128 | tf_op jit(solution)/shard_map/psum | solution.py:125
  760.8 1.6 multiply_subtract_fusion
  762.3 1.3 copy.63
  763.6 1.3 copy.64
  (119 shorter events, 25.1 us)
Async XLA Ops:
  7.2 17.4 %copy-start = (f32[8,128,128]{2,1,0:T(8,128)S(1)}, f32[8,128,128]{2,1,0:T(8,128)}, u32[]{:S(2)}) copy-start(f32[8,128,128]{2,1,0:T(8,128)} %param.8) | copy-start | bytes 1572868
  7.2 211.1 %all-reduce.5.cloned.1.call-start = ((), (), s32[]{:S(2)}) async-start(), calls=%async_computation | async-start | bytes 524288 | tf_op jit(solution)/shard_map/psum | solution.py:89
  8.0 57.3 %collective-permute-start = (s32[16]{0:T(128)S(1)}, s32[16]{0:T(128)S(1)}, u32[]{:S(2)}, u32[]{:S(2)}) collective-permute-start(s32[16]{0:T(128)S(1)} %slice_bitcast_fusion.10), channel_id=1, source_target_pairs={{8,0},{16,8},{24,16},{32,24},{40,32},{48,40},{56,48},{64,56},{72,6... | collective-permute-start | bytes 200 | tf_op jit(solution)/shard_map/ppermute | solution.py:28
  15.6 56.7 %copy-start.6 = (s32[128]{0:T(128)}, s32[128]{0:T(128)S(1)}, u32[]{:S(2)}) copy-start(s32[128]{0:T(128)S(1)} %reshape.186) | copy-start | bytes 1540
  28.8 4.3 copy-start.1
  33.1 17.7 %slice-start = ((s8[8388608]{0:T(1024)(128)(4,1)}), s8[4194304]{0:T(1024)(128)(4,1)S(1)}, s32[]{:S(2)}) async-start(s8[8388608]{0:T(1024)(128)(4,1)} %bitcast.126), calls=%async_computation.1 | async-start | bytes 8388608
  33.8 17.1 %slice-start.1 = ((s8[8388608]{0:T(1024)(128)(4,1)}), s8[4194304]{0:T(1024)(128)(4,1)S(1)}, s32[]{:S(2)}) async-start(s8[8388608]{0:T(1024)(128)(4,1)} %bitcast.126), calls=%async_computation.2 | async-start | bytes 8388608
  279.8 1.2 copy-start.3
  283.8 3.8 collective-permute-start.1
  285.7 5.9 collective-permute-start.2
  291.6 27.0 %collective-permute-start.3 = (f32[16,10,1,128]{3,0,2,1:T(8,128)S(1)}, f32[16,10,1,128]{3,0,2,1:T(8,128)S(1)}, u32[]{:S(2)}, u32[]{:S(2)}) collective-permute-start(f32[16,10,1,128]{3,0,2,1:T(8,128)S(1)} %get-tuple-element.44), channel_id=1, source_target_pairs={{0,1},{1,2},{2,3},{3,4},{4,5},{5,6},{6,7},{8,9},{9,10},{10,11},{11... | collective-permute-start | bytes 245768 | tf_op jit(solution)/shard_map/ppermute | solution.py:19
  301.4 17.3 %collective-permute-start.4 = (f32[16,10,1,128]{3,0,2,1:T(8,128)S(1)}, f32[16,10,1,128]{3,0,2,1:T(8,128)S(1)}, u32[]{:S(2)}, u32[]{:S(2)}) collective-permute-start(f32[16,10,1,128]{3,0,2,1:T(8,128)S(1)} %get-tuple-element.45), channel_id=1, source_target_pairs={{1,0},{2,1},{3,2},{4,3},{5,4},{6,5},{7,6},{9,8},{10,9},{11,10},{12... | collective-permute-start | bytes 245768 | tf_op jit(solution)/shard_map/ppermute | solution.py:20
  397.6 2.1 copy-start.7
  397.6 2.1 copy-start.4
  397.6 17.9 %slice-start.2 = ((s8[8388608]{0:T(1024)(128)(4,1)}), s8[4194304]{0:T(1024)(128)(4,1)S(1)}, s32[]{:S(2)}) async-start(s8[8388608]{0:T(1024)(128)(4,1)} %bitcast.128), calls=%async_computation.3 | async-start | bytes 8388608
  399.7 15.8 %slice-start.3 = ((s8[8388608]{0:T(1024)(128)(4,1)}), s8[4194304]{0:T(1024)(128)(4,1)S(1)}, s32[]{:S(2)}) async-start(s8[8388608]{0:T(1024)(128)(4,1)} %bitcast.128), calls=%async_computation.4 | async-start | bytes 8388608
  415.5 234.6 %copy-start.2 = (f32[128,16,128]{2,1,0:T(8,128)}, f32[128,16,128]{2,1,0:T(8,128)S(1)}, u32[]{:S(2)}) copy-start(f32[128,16,128]{2,1,0:T(8,128)S(1)} %get-tuple-element.72) | copy-start | bytes 3145732
  652.8 108.0 %copy-start.5 = (f32[16]{0:T(128)S(1)}, f32[16]{0:T(128)}, u32[]{:S(2)}) copy-start(f32[16]{0:T(128)} %copy-done.4) | copy-start | bytes 196
  652.8 5.8 collective-permute-start.5
  656.5 5.7 collective-permute-start.6
  662.3 21.6 %collective-permute-start.7 = (f32[16,10,1,128]{3,0,2,1:T(8,128)S(1)}, f32[16,10,1,128]{3,0,2,1:T(8,128)S(1)}, u32[]{:S(2)}, u32[]{:S(2)}) collective-permute-start(f32[16,10,1,128]{3,0,2,1:T(8,128)S(1)} %get-tuple-element.42), channel_id=1, source_target_pairs={{0,1},{1,2},{2,3},{3,4},{4,5},{5,6},{6,7},{8,9},{9,10},{10,11},{11... | collective-permute-start | bytes 245768 | tf_op jit(solution)/shard_map/ppermute | solution.py:19
  666.5 17.3 %collective-permute-start.8 = (f32[16,10,1,128]{3,0,2,1:T(8,128)S(1)}, f32[16,10,1,128]{3,0,2,1:T(8,128)S(1)}, u32[]{:S(2)}, u32[]{:S(2)}) collective-permute-start(f32[16,10,1,128]{3,0,2,1:T(8,128)S(1)} %get-tuple-element.43), channel_id=1, source_target_pairs={{1,0},{2,1},{3,2},{4,3},{5,4},{6,5},{7,6},{9,8},{10,9},{11,10},{12... | collective-permute-start | bytes 245768 | tf_op jit(solution)/shard_map/ppermute | solution.py:20
Sparse Core Ops, SparseCore 0:
  72.0 146.2 all-reduce.4
where the time goes:
time: 779 us; the launch traced here: 772 us
  blocking collectives  483 us (62%)
  matrix products  97.2 us (12%)
  other arithmetic  82.4 us (11%)
  waiting for transfers between devices  32.8 us (4%)
  local copies, waits for them, and re-layouts  30.2 us (4%)
  starting transfers between devices  27.3 us (4%)
  between operations  18.8 us (2%)
    psum x2, blocking collectives, coarse_part(): gathered = lax.psum(local, 'row')  231 us
    psum x2, blocking collectives, alignment_sum(): return lax.psum(jnp.sum(residual * zeta, axis=(1, 2, 3)), ('row', 'col'))  177 us
    dot_general x6, matrix products, block_products(): jnp.einsum('bij,sbj->sbi', picked, flat, precision=lax.Precision.HIGHEST)  91.1 us
    psum x1, blocking collectives, on_device(): lax.psum(jnp.sum(direction * image, axis=(1, 2, 3)), ('row', 'col'))  75.4 us
    another operation x6, other arithmetic, on_device(): factor = jnp.linalg.cholesky(coarse_matrix)  33.9 us
    psum x1, waiting for transfers between devices, on_device(): coarse_matrix = lax.psum(local_matrix + cross_matrix, 'row')  23.7 us
    another operation x6, other arithmetic, coarse_part(): solved = jax.scipy.linalg.cho_solve((factor, True), gathered)  19.9 us
    ppermute x4, starting transfers between devices, padded_2(): before = lax.ppermute(last, axis, up)  19.5 us
  transfers between devices with their start and end apart: 10, of which 5 were waited for; matrix products, arithmetic and copies ran while one was open for 11% of the time, Pallas kernels for 0%

commit v1 on v0

--- a/solution.py
+++ b/solution.py
@@ -100,7 +100,7 @@
     def coarse_part(residual):
         sums = residual.sum(-1).reshape(sizings, blocks).T
         local = jax.ops.segment_sum(sums, flat_ids, num_segments=count)
-        gathered = lax.psum(local, "row")
+        gathered = lax.all_gather(local, "row").sum(axis=0)
         solved = jax.scipy.linalg.cho_solve((factor, True), gathered)
         return solved[flat_ids].T.reshape(sizings, rows_local, cols_local)[..., None]
 

time: 779 us -> 708 us (0.909)
  blocking collectives: 483 us -> 342 us
  waiting for transfers between devices: 32.8 us -> 95.5 us
    psum x2 -> x0, blocking collectives: 231 us -> none  [coarse_part(): gathered = lax.psum(local, 'row')]
    all_gather x0 -> x2, blocking collectives: none -> 105 us  [coarse_part(): gathered = lax.all_gather(local, 'row').sum(axis=0)]
    psum x1, waiting for transfers between devices: 23.7 us -> 86.4 us  [on_device(): coarse_matrix = lax.psum(local_matrix + cross_matrix, 'row')]
    psum x2, blocking collectives: 177 us -> 161 us  [alignment_sum(): return lax.psum(jnp.sum(residual * zeta, axis=(1, 2, 3)), ('row', 'col'))]
  transfers between devices with their start and end apart: 10 -> 10, of which waited for: 5 -> 5; matrix products, arithmetic and copies ran while one was open for 11% -> 13% of each run, Pallas kernels for 0% -> 0%
where the time goes in v1:
time: 708 us; the launch traced here: 701 us
  blocking collectives  342 us (48%)
  matrix products  101 us (14%)
  waiting for transfers between devices  95.5 us (13%)
  other arithmetic  87.3 us (12%)
  local copies, waits for them, and re-layouts  29.6 us (4%)
  starting transfers between devices  26.3 us (4%)
  between operations  18.9 us (3%)
    psum x2, blocking collectives, alignment_sum(): return lax.psum(jnp.sum(residual * zeta, axis=(1, 2, 3)), ('row', 'col'))  161 us
    all_gather x2, blocking collectives, coarse_part(): gathered = lax.all_gather(local, 'row').sum(axis=0)  105 us
    dot_general x6, matrix products, block_products(): jnp.einsum('bij,sbj->sbi', picked, flat, precision=lax.Precision.HIGHEST)  94.4 us
    psum x1, waiting for transfers between devices, on_device(): coarse_matrix = lax.psum(local_matrix + cross_matrix, 'row')  86.4 us
    psum x1, blocking collectives, on_device(): lax.psum(jnp.sum(direction * image, axis=(1, 2, 3)), ('row', 'col'))  76.1 us
    another operation x6, other arithmetic, on_device(): factor = jnp.linalg.cholesky(coarse_matrix)  34 us
    another operation x6, other arithmetic, coarse_part(): solved = jax.scipy.linalg.cho_solve((factor, True), gathered)  19.8 us
    ppermute x4, starting transfers between devices, padded_2(): before = lax.ppermute(last, axis, up)  18.6 us
  transfers between devices with their start and end apart: 10, of which 5 were waited for; matrix products, arithmetic and copies ran while one was open for 13% of the time, Pallas kernels for 0%

profile of v1, /device:TPU:1, one launch (start us, length us, event | category | flops | bytes accessed | tf_op | source)
XLA Modules:
  0.0 700.9 jit_solution(17341688851037991283)
XLA Ops:
  8.0 1.3 collective-permute-start
  11.6 1.4 slice_reduce_fusion.1
  18.7 5.8 copy.63
  25.6 4.3 gather_fusion.2
  29.9 1.8 gather_fusion
  31.8 1.2 gather_fusion.3
  34.4 16.3 %fusion.50 = f32[128,16,128]{2,1,0:T(8,128)S(1)} fusion(f32[16,128,128]{2,0,1:T(8,128)S(1)} %bitcast.141, f32[128,128,128]{2,1,0:T(8,128)} %gather_fusion.2), kind=kOutput, calls=%fused_computation.144 | convolution fusion | flops 402653184 | bytes 10485760 | tf_op jit(solution)/shard_map/bij,sbj->sbi/dot_general | solution.py:75
  51.4 14.2 %fusion.51 = f32[128,16,128]{2,1,0:T(8,128)} fusion(f32[16,128,128]{2,0,1:T(8,128)S(1)} %bitcast.142, f32[128,128,128]{2,1,0:T(8,128)S(1)} %bitcast.129), kind=kOutput, calls=%fused_computation.145 | convolution fusion | flops 402653184 | bytes 10485760 | tf_op jit(solution)/shard_map/bij,sbj->sbi/dot_general | solution.py:75
  67.8 4.7 scatter_custom_fusion
  73.5 57.6 %all-gather = f32[8192,16]{1,0:T(8,128)} all-gather(f32[256,16]{1,0:T(8,128)S(1)} %scatter_custom_fusion.1), channel_id=2, replica_groups=mesh['row'=32,'col'=8] {'row'}, dimensions={0}, use_global_device_ids=true | all-gather | bytes 540672 | tf_op jit(solution)/shard_map/all_gather | solution.py:103
  131.1 2.5 reduce_sum.103
  133.7 86.4 %all-reduce.5.cloned.1.call-done = f32[256,256]{0,1:T(8,128)} async-done(((f32[256,256]{0,1:T(8,128)}), f32[256,256]{0,1:T(8,128)}) %all-reduce.5.cloned.1.call-update) | async-done | bytes 262160 | tf_op jit(solution)/shard_map/psum | solution.py:89
  222.2 11.7 %cholesky.50 = f32[128,128]{1,0:T(8,128)S(1)} custom-call(f32[128,128]{1,0:T(8,128)S(1)} %cholesky.118), custom_call_target="Cholesky" | custom-call | tf_op jit(solution)/shard_map/jit(cholesky)/cholesky | solution.py:90
  234.0 9.8 %custom-call.16 = f32[1,128,128]{1,2,0:T(8,128)S(1)} custom-call(f32[1,128,128]{2,1,0:T(8,128)S(1)} %get-tuple-element.57), custom_call_target="InvertDiagBlocksLowerTriangular" | custom-call | tf_op jit(solution)/shard_map/jit(cholesky)/cholesky | solution.py:90
  244.3 11.7 %cholesky.105 = f32[128,128]{1,0:T(8,128)S(1)} custom-call(f32[128,128]{1,0:T(8,128)S(1)} %convolution_subtract_fusion), custom_call_target="Cholesky" | custom-call | tf_op jit(solution)/shard_map/jit(cholesky)/cholesky | solution.py:90
  258.1 4.1 while.4
  258.9 1.4 bitcast_dynamic-update-slice_fusion.2
  260.9 1.4 bitcast_dynamic-update-slice_fusion.2
  262.2 19.7 %custom-call.20 = f32[2,128,128]{1,2,0:T(8,128)S(1)} custom-call(f32[2,128,128]{2,1,0:T(8,128)S(1)} %get-tuple-element.17), custom_call_target="InvertDiagBlocksLowerTriangular" | custom-call | tf_op jit(solution)/shard_map/jit(_cho_solve)/triangular_solve | solution.py:104
  284.0 2.0 add_add_fusion.1
  286.0 1.8 collective-permute-start.1
  287.8 1.3 collective-permute-start.2
  289.8 4.0 collective-permute-done.2
  293.8 9.8 %collective-permute-start.3 = (f32[16,10,1,128]{3,0,2,1:T(8,128)S(1)}, f32[16,10,1,128]{3,0,2,1:T(8,128)S(1)}, u32[]{:S(2)}, u32[]{:S(2)}) collective-permute-start(f32[16,10,1,128]{3,0,2,1:T(8,128)S(1)} %get-tuple-element.46), channel_id=1, source_target_pairs={{0,1},{1,2},{2,3},{3,4},{4,5},{5,6},{6,7},{8,9},{9,10},{10,11},{11... | collective-permute-start | bytes 245768 | tf_op jit(solution)/shard_map/ppermute | solution.py:19
  303.6 1.9 collective-permute-start.4
  305.5 15.4 %fusion.52 = f32[128,16,128]{2,1,0:T(8,128)S(1)} fusion(f32[16,128,128]{2,0,1:T(8,128)S(1)} %bitcast.130, f32[128,128,128]{2,1,0:T(8,128)} %gather_fusion.2), kind=kOutput, calls=%fused_computation.146 | convolution fusion | flops 402653184 | bytes 10485760 | tf_op jit(solution)/shard_map/bij,sbj->sbi/dot_general | solution.py:75
  320.9 1.8 multiply_reduce_fusion.2
  322.7 77.3 %all-reduce.2 = (f32[16]{0:T(128)S(1)}, f32[16]{0:T(128)S(1)}) all-reduce(f32[16]{0:T(128)S(1)} %get-tuple-element.24, f32[16]{0:T(128)S(1)} %get-tuple-element.23), channel_id=1, replica_groups=mesh['row'=32,'col'=8] {'row','col'}, use_global_device_ids=true, to_apply=%region_13.15 | all-reduce | flops 32 | bytes 256 | tf_op jit(solution)/shard_map/psum | solution.py:58
  400.0 1.9 broadcast_divide_fusion
  402.0 16.2 %divide_add_fusion = (f32[16,8,16,128]{3,0,2,1:T(8,128)}, f32[16,8,16]{0,2,1:T(8,128)S(1)}, f32[128,16,128]{2,1,0:T(8,128)S(1)}) fusion(f32[16,8,16,128]{3,0,2,1:T(8,128)S(1)} %get-tuple-element.40, f32[128]{0:T(128)S(1)} %add_multiply_fusion, f32[8,16,128]{2,1,0:T(8,128)S(1)} %broadcast_add_fusion, f32[16,128,128]{2,0,1:T(8,128)S(1)} %bitcast.140, ...), kind=kOutput, calls=%fused_computation.54 | convolution fusion | flops 404486144 | bytes 12657152 | tf_op jit(solution)/shard_map/bij,sbj->sbi/dot_general | solution.py:75
  418.2 1.8 scatter_custom_fusion.2
  420.0 47.3 %all-gather.1 = f32[8192,16]{1,0:T(8,128)} all-gather(f32[256,16]{1,0:T(8,128)} %scatter_custom_fusion.2), channel_id=3, replica_groups=mesh['row'=32,'col'=8] {'row'}, dimensions={0}, use_global_device_ids=true | all-gather | bytes 540672 | tf_op jit(solution)/shard_map/all_gather | solution.py:103
  467.2 3.1 reduce_sum.107
  471.5 16.6 %fusion.53 = f32[128,16,128]{2,1,0:T(8,128)} fusion(f32[16,128,128]{2,0,1:T(8,128)} %bitcast.139, f32[128,128,128]{2,1,0:T(8,128)} %gather_fusion.2), kind=kOutput, calls=%fused_computation.147 | convolution fusion | flops 402653184 | bytes 10485760 | tf_op jit(solution)/shard_map/bij,sbj->sbi/dot_general | solution.py:75
  492.6 1.9 multiply_reduce_fusion.1
  494.5 84.1 %psum.38 = f32[16]{0:T(128)S(1)} all-reduce(f32[16]{0:T(128)S(1)} %multiply_reduce_fusion.1), channel_id=1, replica_groups=mesh['row'=32,'col'=8] {'row','col'}, use_global_device_ids=true, to_apply=%region_20.22 | all-reduce | flops 16 | bytes 128 | tf_op jit(solution)/shard_map/psum | solution.py:58
  579.3 2.1 multiply_add_fusion.1
  581.4 3.3 collective-permute-start.5
  584.8 1.3 collective-permute-start.6
  586.9 3.6 collective-permute-done.6
  590.5 3.7 collective-permute-start.7
  594.2 1.9 collective-permute-start.8
  596.1 15.7 %fusion.54 = f32[128,16,128]{2,1,0:T(8,128)S(1)} fusion(f32[16,128,128]{2,0,1:T(8,128)S(1)} %bitcast.131, f32[128,128,128]{2,1,0:T(8,128)} %gather_fusion.2), kind=kOutput, calls=%fused_computation.148 | convolution fusion | flops 402653184 | bytes 10485760 | tf_op jit(solution)/shard_map/bij,sbj->sbi/dot_general | solution.py:75
  611.8 1.5 multiply_reduce_fusion
  613.3 76.1 %psum.39 = f32[16]{0:T(128)S(1)} all-reduce(f32[16]{0:T(128)S(1)} %get-tuple-element.37), channel_id=1, replica_groups=mesh['row'=32,'col'=8] {'row','col'}, use_global_device_ids=true, to_apply=%region_22.24 | all-reduce | flops 16 | bytes 128 | tf_op jit(solution)/shard_map/psum | solution.py:125
  689.4 1.6 multiply_subtract_fusion
  690.9 1.3 copy.80
  692.2 1.3 copy.79
  (129 shorter events, 27.0 us)
Async XLA Ops:
  7.2 17.3 %copy-start = (f32[8,128,128]{2,1,0:T(8,128)S(1)}, f32[8,128,128]{2,1,0:T(8,128)}, u32[]{:S(2)}) copy-start(f32[8,128,128]{2,1,0:T(8,128)} %param.8) | copy-start | bytes 1572868
  7.2 18.0 %copy-start.1 = (f32[16,8,16,128]{3,2,1,0:T(8,128)S(1)}, f32[16,8,16,128]{3,2,1,0:T(8,128)}, u32[]{:S(2)}) copy-start(f32[16,8,16,128]{3,2,1,0:T(8,128)} %param.7) | copy-start | bytes 3145732
  7.2 212.9 %all-reduce.5.cloned.1.call-start = ((), (), s32[]{:S(2)}) async-start(), calls=%async_computation | async-start | bytes 524288 | tf_op jit(solution)/shard_map/psum | solution.py:89
  8.0 58.9 %collective-permute-start = (s32[16]{0:T(128)S(1)}, s32[16]{0:T(128)S(1)}, u32[]{:S(2)}, u32[]{:S(2)}) collective-permute-start(s32[16]{0:T(128)S(1)} %slice_bitcast_fusion.10), channel_id=1, source_target_pairs={{8,0},{16,8},{24,16},{32,24},{40,32},{48,40},{56,48},{64,56},{72,6... | collective-permute-start | bytes 200 | tf_op jit(solution)/shard_map/ppermute | solution.py:28
  11.6 390.3 %copy-start.4 = (f32[128]{0:T(128)}, f32[128]{0:T(128)S(1)}, u32[]{:S(2)}) copy-start(f32[128]{0:T(128)S(1)} %add_multiply_fusion) | copy-start | bytes 1540
  13.0 307.9 %copy-start.6 = (f32[128]{0:T(128)}, f32[128]{0:T(128)S(1)}, u32[]{:S(2)}) copy-start(f32[128]{0:T(128)S(1)} %get-tuple-element.64) | copy-start | bytes 1540
  13.0 307.9 %copy-start.8 = (f32[128]{0:T(128)}, f32[128]{0:T(128)S(1)}, u32[]{:S(2)}) copy-start(f32[128]{0:T(128)S(1)} %get-tuple-element.65) | copy-start | bytes 1540
  33.7 17.7 %slice-start = ((s8[8388608]{0:T(1024)(128)(4,1)}), s8[4194304]{0:T(1024)(128)(4,1)S(1)}, s32[]{:S(2)}) async-start(s8[8388608]{0:T(1024)(128)(4,1)} %bitcast.128), calls=%async_computation.1 | async-start | bytes 8388608
  34.3 17.1 %slice-start.1 = ((s8[8388608]{0:T(1024)(128)(4,1)}), s8[4194304]{0:T(1024)(128)(4,1)S(1)}, s32[]{:S(2)}) async-start(s8[8388608]{0:T(1024)(128)(4,1)} %bitcast.128), calls=%async_computation.2 | async-start | bytes 8388608
  133.7 150.2 %copy-start.5 = (s32[1024]{0:T(1024)}, s32[1024]{0:T(1024)S(1)}, u32[]{:S(2)}) copy-start(s32[1024]{0:T(1024)S(1)} %pad_clamp_fusion) | copy-start | bytes 12292
  281.9 1.2 copy-start.3
  286.0 3.7 collective-permute-start.1
  287.8 5.9 collective-permute-start.2
  293.8 27.1 %collective-permute-start.3 = (f32[16,10,1,128]{3,0,2,1:T(8,128)S(1)}, f32[16,10,1,128]{3,0,2,1:T(8,128)S(1)}, u32[]{:S(2)}, u32[]{:S(2)}) collective-permute-start(f32[16,10,1,128]{3,0,2,1:T(8,128)S(1)} %get-tuple-element.46), channel_id=1, source_target_pairs={{0,1},{1,2},{2,3},{3,4},{4,5},{5,6},{6,7},{8,9},{9,10},{10,11},{11... | collective-permute-start | bytes 245768 | tf_op jit(solution)/shard_map/ppermute | solution.py:19
  303.6 17.3 %collective-permute-start.4 = (f32[16,10,1,128]{3,0,2,1:T(8,128)S(1)}, f32[16,10,1,128]{3,0,2,1:T(8,128)S(1)}, u32[]{:S(2)}, u32[]{:S(2)}) collective-permute-start(f32[16,10,1,128]{3,0,2,1:T(8,128)S(1)} %get-tuple-element.47), channel_id=1, source_target_pairs={{1,0},{2,1},{3,2},{4,3},{5,4},{6,5},{7,6},{9,8},{10,9},{11,10},{12... | collective-permute-start | bytes 245768 | tf_op jit(solution)/shard_map/ppermute | solution.py:20
  400.0 18.2 %copy-start.12 = (f32[16]{0:T(128)}, f32[16]{0:T(128)S(1)}, u32[]{:S(2)}) copy-start(f32[16]{0:T(128)S(1)} %get-tuple-element.35) | copy-start | bytes 196
  400.0 1.9 copy-start.10
  418.2 74.5 %copy-start.2 = (f32[128,16,128]{2,1,0:T(8,128)}, f32[128,16,128]{2,1,0:T(8,128)S(1)}, u32[]{:S(2)}) copy-start(f32[128,16,128]{2,1,0:T(8,128)S(1)} %get-tuple-element.74) | copy-start | bytes 3145732
  470.4 17.8 %slice-start.2 = ((f32[256,16]{1,0:T(8,128)}), f32[128,16]{1,0:T(8,128)S(1)}, s32[]{:S(2)}) async-start(f32[256,16]{1,0:T(8,128)} %reduce_sum.107), calls=%async_computation.3 | async-start | bytes 131072 | tf_op jit(solution)/shard_map/jit(_cho_solve)/triangular_solve | solution.py:104
  579.3 32.5 %copy-start.7 = (f32[128]{0:T(128)S(1)}, f32[128]{0:T(128)}, u32[]{:S(2)}) copy-start(f32[128]{0:T(128)} %copy-done.6) | copy-start | bytes 1540
  579.3 32.6 %copy-start.9 = (f32[128]{0:T(128)S(1)}, f32[128]{0:T(128)}, u32[]{:S(2)}) copy-start(f32[128]{0:T(128)} %copy-done.8) | copy-start | bytes 1540
  581.4 108.0 %copy-start.11 = (f32[16]{0:T(128)S(1)}, f32[16]{0:T(128)}, u32[]{:S(2)}) copy-start(f32[16]{0:T(128)} %copy-done.10) | copy-start | bytes 196
  581.4 5.5 collective-permute-start.5
  584.8 5.7 collective-permute-start.6
  590.5 21.3 %collective-permute-start.7 = (f32[16,10,1,128]{3,0,2,1:T(8,128)S(1)}, f32[16,10,1,128]{3,0,2,1:T(8,128)S(1)}, u32[]{:S(2)}, u32[]{:S(2)}) collective-permute-start(f32[16,10,1,128]{3,0,2,1:T(8,128)S(1)} %get-tuple-element.44), channel_id=1, source_target_pairs={{0,1},{1,2},{2,3},{3,4},{4,5},{5,6},{6,7},{8,9},{9,10},{10,11},{11... | collective-permute-start | bytes 245768 | tf_op jit(solution)/shard_map/ppermute | solution.py:19
  594.2 17.6 %collective-permute-start.8 = (f32[16,10,1,128]{3,0,2,1:T(8,128)S(1)}, f32[16,10,1,128]{3,0,2,1:T(8,128)S(1)}, u32[]{:S(2)}, u32[]{:S(2)}) collective-permute-start(f32[16,10,1,128]{3,0,2,1:T(8,128)S(1)} %get-tuple-element.45), channel_id=1, source_target_pairs={{1,0},{2,1},{3,2},{4,3},{5,4},{6,5},{7,6},{9,8},{10,9},{11,10},{12... | collective-permute-start | bytes 245768 | tf_op jit(solution)/shard_map/ppermute | solution.py:20
Sparse Core Ops, SparseCore 0:
  73.6 146.4 all-reduce.4
